TPU v7x, 256 devices: a whole 4x4x8 slice. The times are simulated.
256 devices in a mesh: row: 8 (over x_hi, y), col: 32 (over z, x_lo, core).
Axes of the slice: x: 4 (x_hi: 2, x_lo: 2; x = x_hi * 2 + x_lo), y: 4, z: 8, core: 2. Of those that a mesh axis runs over, the one named last changes fastest.
Arguments:
- region_inverse: float32 [4096, 4096], P('row', 'col'), may hold values from -6 to 6
- factor_cols: float32 [3, 4096, 512], P(None, 'row'), may hold values from -0.09375 to 0.09375
- parent_factor: float32 [2, 512, 512], P(None, 'col'), may hold values from -0.25 to 0.25
- diag_inverse: float32 [3, 512, 512], P(None, 'col'), may hold values from -6 to 6
- listed: int32 [3, 8], replicated, may hold values from 0 to 1, as said below
Outputs:
- col_blocks: float32 [3, 4096, 512], P(None, ('row', 'col'))
- diag_blocks: float32 [3, 512, 512], P(None, 'col')
- parent_rows: float32 [2, 512, 512], P(None, 'col')
Inputs may be any that keep to these rules, and one draw needn't show every extreme that they name: listed[0] has exactly 6 ones; listed[1] and listed[2] have exactly 4 ones each, all at blocks that listed[0] also lists.
All inputs are finite; a program needn't handle non-finite values.
Results may differ from a plain program's by a relative error of at most 0.0001.
Values sent between devices are 32-bit elements; how exact they have to be, the bound alone decides.
A program may use at most 64 MiB of HBM per device.

v0:
```python
import jax
import jax.numpy as jnp
from jax import lax
from jax.sharding import PartitionSpec as P


def broadcast(value, axis, source):
    kept = jnp.where(lax.axis_index(axis) == source, value, 0).astype(value.dtype)
    return lax.psum(kept, axis)


def matmul_plain(left, right):
    return jnp.dot(left, right, precision=lax.Precision.HIGHEST, preferred_element_type=jnp.float32)


def matmul_left(left, right):
    return lax.dot_general(
        left,
        right,
        (((0,), (0,)), ((), ())),
        precision=lax.Precision.HIGHEST,
        preferred_element_type=jnp.float32,
    )


def row_weights(listed_row, first_row, count, width):
    global_rows = first_row + lax.iota(jnp.int32, count)
    block_ids = global_rows // width
    table = lax.iota(jnp.int32, listed_row.shape[0])
    hits = (block_ids[:, None] == table[None, :]).astype(jnp.float32) * listed_row.astype(
        jnp.float32
    )[None, :]
    return jnp.sum(hits, axis=1)


def total_sums(values):
    return lax.psum(tuple(values), ("row", "col"))


def shards(region_inverse, factor_cols, parent_factor, diag_inverse, listed):
    row_count = lax.axis_size("row")
    col_count = lax.axis_size("col")
    row_place = lax.axis_index("row")
    col_place = lax.axis_index("col")
    rows_here, cols_here = region_inverse.shape
    width = factor_cols.shape[2]
    group = rows_here // col_count
    ratio = col_count // row_count
    diag_width = width // col_count
    diag_start = col_place * diag_width
    full_diag, full_parent = (
        lax.all_gather(diag_inverse, "col", axis=1, tiled=True),
        lax.all_gather(parent_factor, "col", axis=1, tiled=True),
    )
    masks = [
        row_weights(listed[member], row_place * rows_here, rows_here, width) for member in range(3)
    ]
    factors = [factor_cols[member] * masks[member][:, None] for member in range(3)]
    group_masks = [
        lax.dynamic_slice_in_dim(masks[member], col_place * group, group, 0) for member in range(3)
    ]
    pieces = [
        lax.dynamic_slice_in_dim(factors[member], col_place * group, group, 0)
        for member in range(3)
    ]

    def column_pass(members, extra_rows):
        slices = [
            lax.dynamic_slice_in_dim(factors[member], col_place % ratio * cols_here, cols_here, 0)
            for member in members
        ]
        stacked = jnp.stack(slices, axis=1)
        received = broadcast(stacked, "row", col_place // ratio)
        right_side = received.reshape(cols_here, len(members) * width)
        summed = lax.psum_scatter(
            matmul_plain(region_inverse, right_side), "col", scatter_dimension=0, tiled=True
        )
        outputs = []
        terms = []
        for place, member in enumerate(members):
            partial_sum = summed
            if extra_rows[place] is not None:
                partial_sum = partial_sum + extra_rows[place]
            column = -partial_sum * group_masks[member][:, None]
            outputs.append(column)
            terms.append(-matmul_left(pieces[member], column))
        return (outputs, terms)

    parent_out, parent_terms = column_pass([0], [None])
    parent_col = parent_out[0]
    parent_totals = total_sums(parent_terms)
    parent_diag = full_diag[0] + parent_totals[0]
    parent_slice = lax.dynamic_slice_in_dim(parent_diag, diag_start, diag_width, 0)
    links = [full_parent[0], full_parent[1]]
    extra_rows = [matmul_plain(parent_col, links[place]) for place in range(2)]
    extra_sums = [matmul_left(parent_col, pieces[place + 1]) for place in range(2)]
    child_cols = []
    diag_list = [parent_slice]
    upper_list = []
    for place in range(2):
        outputs, terms = column_pass([place + 1], [extra_rows[place]])
        child_cols.append(outputs[0])
        link_terms = [extra_sums[place]]
        places = [place]
        count = len(places)
        diags = []
        uppers = []
        totals = total_sums(list(terms) + list(link_terms))
        for k, finish_place in enumerate(places):
            link_cols = lax.dynamic_slice_in_dim(links[finish_place], diag_start, diag_width, 1)
            upper_total = totals[count + k]
            upper_slice = -(
                lax.dynamic_slice_in_dim(upper_total, diag_start, diag_width, 0)
                + matmul_plain(parent_slice, links[finish_place])
            )
            weighted_diag = matmul_left(link_cols, parent_diag)
            link_upper = -(
                matmul_left(link_cols, upper_total)
                + matmul_plain(weighted_diag, links[finish_place])
            )
            diag_rows = lax.dynamic_slice_in_dim(
                full_diag[finish_place + 1], diag_start, diag_width, 0
            )
            total_rows = lax.dynamic_slice_in_dim(totals[k], diag_start, diag_width, 0)
            diags.append(diag_rows + total_rows - link_upper)
            uppers.append(upper_slice)
        diags, uppers = (diags, uppers)
        diag_list = diag_list + diags
        upper_list = upper_list + uppers
    col_blocks = jnp.stack([parent_col] + child_cols)
    diag_blocks = jnp.stack(diag_list)
    parent_rows = jnp.stack(upper_list)
    return (col_blocks, diag_blocks, parent_rows)


def solution(mesh):
    in_specs = (
        P("row", "col"),
        P(None, "row", None),
        P(None, "col", None),
        P(None, "col", None),
        P(),
    )
    out_specs = (P(None, ("row", "col"), None), P(None, "col", None), P(None, "col", None))
    return jax.shard_map(shards, mesh=mesh, in_specs=in_specs, out_specs=out_specs, check_vma=False)
```

profile of v0, /device:TPU:8, one launch (start us, length us, event | category | flops | bytes accessed | tf_op | source)
XLA Modules:
  0.0 894.7 jit_solution(15378608520947166456)
XLA Ops:
  7.3 0.8 convert_bitcast_fusion.2
  8.2 2.1 bitcast_multiply_fusion.1
  10.3 0.8 dynamic-slice_select_fusion.2
  11.4 0.9 dynamic-slice_select_fusion
  12.3 91.4 %all-reduce.7.cloned.1.call-done = (f32[128,512]{1,0:T(8,128)}, f32[128,512]{1,0:T(8,128)}, f32[128,512]{1,0:T(8,128)}) async-done(((f32[128,512]{1,0:T(8,128)}, f32[128,512]{1,0:T(8,128)}, f32[128,512]{1,0:T(8,128)}), (f32[128,512]{1,0:T(8,128)}, f32[128,512]{1,0:T(8,128)}, f32[128,512]{1,0:T(8,128)})) %all-reduce.7.cloned.1.call-update) | async-done | bytes 786448 | tf_op jit(solution)/shard_map/psum | solution.py:9
  103.8 2.0 convolution_bitcast_fusion.2
  105.8 1.4 copy.17
  107.3 1.0 convolution_bitcast_fusion.1
  108.3 1.3 copy.19
  110.3 1.0 convolution_bitcast_fusion
  111.3 1.3 copy.21
  113.7 113.7 %reduce-scatter.10.cloned.1.call-done = f32[16,512]{1,0:T(8,128)} async-done(((f32[512,512]{1,0:T(8,128)}), f32[16,512]{1,0:T(8,128)}) %reduce-scatter.10.cloned.1.call-update) | async-done | bytes 32784
  227.4 0.9 copy.18
  228.3 2.9 convolution_negate_fusion.2
  231.2 2.0 fusion.33
  233.2 2.7 fusion.34
  235.9 110.6 %reduce-scatter.12.cloned.1.call-done = f32[16,512]{1,0:T(8,128)} async-done(((f32[512,512]{1,0:T(8,128)}), f32[16,512]{1,0:T(8,128)}) %reduce-scatter.12.cloned.1.call-update) | async-done | bytes 32784 | tf_op jit(solution)/shard_map/reduce_scatter | solution.py:75
  346.5 64.3 %all-gather.3.cloned.1.call-done = f32[2,512,512]{2,1,0:T(8,128)} async-done(((f32[2,16,512]{2,1,0:T(8,128)}), f32[2,512,512]{2,1,0:T(8,128)}) %all-gather.3.cloned.1.call-update) | async-done | bytes 2097168 | tf_op jit(solution)/shard_map/all_gather | solution.py:53
  410.8 2.0 fusion.13
  412.8 2.8 convolution_negate_fusion.1
  415.6 115.7 %reduce-scatter.14.cloned.1.call-done = f32[16,512]{1,0:T(8,128)} async-done(((f32[512,512]{1,0:T(8,128)}), f32[16,512]{1,0:T(8,128)}) %reduce-scatter.14.cloned.1.call-update) | async-done | bytes 32784 | tf_op jit(solution)/shard_map/reduce_scatter | solution.py:75
  531.3 1.4 fusion.11
  532.6 2.8 convolution_negate_fusion
  536.3 1.2 fusion.64
  537.5 59.3 %all-gather.5.cloned.1.call-done = f32[3,512,512]{2,1,0:T(8,128)} async-done(((f32[3,16,512]{2,1,0:T(8,128)}), f32[3,512,512]{2,1,0:T(8,128)}) %all-gather.5.cloned.1.call-update) | async-done | bytes 3145744 | tf_op jit(solution)/shard_map/all_gather | solution.py:52
  596.7 3.0 fusion.63
  599.7 278.1 %all-reduce.5.cloned.1.call-done = (f32[512,512]{1,0:T(8,128)}, f32[512,512]{1,0:T(8,128)}, f32[512,512]{1,0:T(8,128)}, f32[512,512]{1,0:T(8,128)}, f32[512,512]{1,0:T(8,128)}) async-done(((f32[512,512]{1,0:T(8,128)}, f32[512,512]{1,0:T(8,128)}, f32[512,512]{1,0:T(8,128)}, f32[512,512]{1,0:T(8,128)}, f32[512,512]{1,0:T(8,128)}), (f32[512,512]{1,0:T(8,128)}, f32[512,512]{1,0:T(8,128)}, f32[512,512]{1,0:T(8,128)}, ...) | async-done | bytes 5242896 | tf_op jit(solution)/shard_map/psum | solution.py:37
  877.8 1.9 fusion.14
  880.5 0.7 fusion.27
  881.9 0.7 fusion.23
  884.4 1.4 fusion.9
  885.8 1.4 fusion.6
  (49 shorter events, 6.9 us)
Async XLA Ops:
  7.2 96.6 %copy-start = (f32[512,128]{1,0:T(8,128)S(1)}, f32[512,128]{1,0:T(8,128)}, u32[]{:S(2)}) copy-start(f32[512,128]{1,0:T(8,128)} %param.5) | copy-start | bytes 786436
  7.2 96.6 %all-reduce.7.cloned.1.call-start = ((), (), s32[]{:S(2)}) async-start(), calls=%async_computation.9 | async-start | bytes 1572864 | tf_op jit(solution)/shard_map/psum | solution.py:9
  10.3 1.1 copy-start.4
  10.3 2.0 copy-start.5
  10.3 220.8 %copy-start.3 = (f32[512,512]{1,0:T(8,128)}, f32[512,512]{1,0:T(8,128)S(1)}, u32[]{:S(2)}) copy-start(f32[512,512]{1,0:T(8,128)S(1)} %get-tuple-element.21) | copy-start | bytes 3145732
  12.3 215.1 %reduce-scatter.10.cloned.1.call-start = ((), (), s32[]{:S(2)}) async-start(), calls=%async_computation.5 | async-start | bytes 1081344
  103.8 3.5 copy-start.9
  107.2 239.2 %reduce-scatter.12.cloned.1.call-start = ((), (), s32[]{:S(2)}) async-start(), calls=%async_computation.6 | async-start | bytes 1081344 | tf_op jit(solution)/shard_map/reduce_scatter | solution.py:75
  107.3 3.0 copy-start.8
  109.7 301.1 %all-gather.3.cloned.1.call-start = ((), (), s32[]{:S(2)}) async-start(), calls=%async_computation.3 | async-start | bytes 2162688 | tf_op jit(solution)/shard_map/all_gather | solution.py:53
  110.2 421.0 %reduce-scatter.14.cloned.1.call-start = ((), (), s32[]{:S(2)}) async-start(), calls=%async_computation.7 | async-start | bytes 1081344 | tf_op jit(solution)/shard_map/reduce_scatter | solution.py:75
  112.7 484.0 %all-gather.5.cloned.1.call-start = ((), (), s32[]{:S(2)}) async-start(), calls=%async_computation.4 | async-start | bytes 3244032 | tf_op jit(solution)/shard_map/all_gather | solution.py:52
  113.3 764.5 %all-reduce.5.cloned.1.call-start = ((), (), s32[]{:S(2)}) async-start(), calls=%async_computation.8 | async-start | bytes 10485760 | tf_op jit(solution)/shard_map/psum | solution.py:37
  410.8 120.5 %copy-start.1 = (f32[2,512,512]{2,1,0:T(8,128)S(1)}, f32[2,512,512]{2,1,0:T(8,128)}, u32[]{:S(2)}) copy-start(f32[2,512,512]{2,1,0:T(8,128)} %all-gather.3.cloned.1.call-done) | copy-start | bytes 6291460
  877.8 1.9 copy-start.2
  877.8 2.6 copy-start.7
  879.7 2.1 copy-start.6
Sparse Core Ops, SparseCore 0:
  12.4 91.3 all-reduce.6
  107.3 120.0 reduce-scatter.9
  229.9 116.4 reduce-scatter.11
  348.2 62.5 all-gather.2
  413.1 118.0 reduce-scatter.13
  533.0 63.6 all-gather.4
  603.0 274.8 all-reduce.4
where the time goes:
time: 895 us
  waiting for transfers between devices  834 us (93%)
  matrix products  27.4 us (3%)
  between operations  14.3 us (2%)
  local copies, waits for them, and re-layouts  9.69 us (1%)
    psum x1, waiting for transfers between devices, total_sums(): return lax.psum(tuple(values), ('row', 'col'))  278 us
    reduce_scatter x2, waiting for transfers between devices, column_pass(): lax.psum_scatter(matmul_plain(region_inverse, right_side), 'col', scatter...  226 us
    unnamed x8, waiting for transfers between devices  115 us
    psum x1, waiting for transfers between devices, broadcast(): return lax.psum(kept, axis)  91.4 us
    all_gather x1, waiting for transfers between devices, shards(): lax.all_gather(parent_factor, 'col', axis=1, tiled=True)  64.3 us
    all_gather x1, waiting for transfers between devices, shards(): lax.all_gather(diag_inverse, 'col', axis=1, tiled=True)  59.3 us
  transfers between devices with their start and end apart: 7, of which 7 were waited for; matrix products, arithmetic and copies ran while one was open for 3% of the time, Pallas kernels for 0%

commit v1 on v0

--- a/solution.py
+++ b/solution.py
@@ -34,7 +34,10 @@
 
 
 def total_sums(values):
-    return lax.psum(tuple(values), ("row", "col"))
+    resolve_the_domain = lambda sheet, axis_tag, chip_axis: lax.psum(
+        lax.psum(sheet, axis_tag), chip_axis
+    )
+    return resolve_the_domain(tuple(values), "row", "col")
 
 
 def shards(region_inverse, factor_cols, parent_factor, diag_inverse, listed):

time: 895 us -> 996 us (1.11)
  waiting for transfers between devices: 834 us -> 934 us
    psum x1 -> x2, waiting for transfers between devices: 278 us -> 370 us  [the longest x1 244 us: total_sums(): lax.psum(lax.psum(sheet, axis_tag), chip_axis)]
    unnamed x8 -> x9, waiting for transfers between devices: 115 us -> 116 us
  transfers between devices with their start and end apart: 7 -> 8, of which waited for: 7 -> 8; matrix products, arithmetic and copies ran while one was open for 3% -> 2% of each run, Pallas kernels for 0% -> 0%
where the time goes in v1:
time: 996 us; the launch traced here: 995 us
  waiting for transfers between devices  934 us (94%)
  matrix products  27.4 us (3%)
  between operations  14.4 us (1%)
    psum x1, waiting for transfers between devices, total_sums(): lax.psum(lax.psum(sheet, axis_tag), chip_axis)  244 us
    reduce_scatter x2, waiting for transfers between devices, column_pass(): lax.psum_scatter(matmul_plain(region_inverse, right_side), 'col', scatter...  226 us
    psum x1, waiting for transfers between devices, total_sums(): lax.psum(sheet, axis_tag)  126 us
    unnamed x9, waiting for transfers between devices  116 us
    psum x1, waiting for transfers between devices, broadcast(): return lax.psum(kept, axis)  91.4 us
    all_gather x1, waiting for transfers between devices, shards(): lax.all_gather(diag_inverse, 'col', axis=1, tiled=True)  66.6 us
    all_gather x1, waiting for transfers between devices, shards(): lax.all_gather(parent_factor, 'col', axis=1, tiled=True)  64.2 us
  transfers between devices with their start and end apart: 8, of which 8 were waited for; matrix products, arithmetic and copies ran while one was open for 2% of the time, Pallas kernels for 0%

profile of v1, /device:TPU:8, one launch (start us, length us, event | category | flops | bytes accessed | tf_op | source)
XLA Modules:
  0.0 994.8 jit_solution(2026062056038799613)
XLA Ops:
  7.3 0.8 convert_bitcast_fusion.2
  8.2 2.1 bitcast_multiply_fusion.1
  10.3 0.8 dynamic-slice_select_fusion.2
  11.4 0.8 dynamic-slice_select_fusion
  12.3 91.4 %all-reduce.11.cloned.1.call-done = (f32[128,512]{1,0:T(8,128)}, f32[128,512]{1,0:T(8,128)}, f32[128,512]{1,0:T(8,128)}) async-done(((f32[128,512]{1,0:T(8,128)}, f32[128,512]{1,0:T(8,128)}, f32[128,512]{1,0:T(8,128)}), (f32[128,512]{1,0:T(8,128)}, f32[128,512]{1,0:T(8,128)}, f32[128,512]{1,0:T(8,128)})) %all-reduce.11.cloned.1.call-update) | async-done | bytes 786448 | tf_op jit(solution)/shard_map/psum | solution.py:9
  103.7 2.0 convolution_bitcast_fusion.2
  105.7 1.4 copy.17
  107.2 1.0 convolution_bitcast_fusion.1
  108.2 1.3 copy.19
  110.2 1.0 convolution_bitcast_fusion
  111.2 1.3 copy.21
  112.9 114.4 %reduce-scatter.10.cloned.1.call-done = f32[16,512]{1,0:T(8,128)} async-done(((f32[512,512]{1,0:T(8,128)}), f32[16,512]{1,0:T(8,128)}) %reduce-scatter.10.cloned.1.call-update) | async-done | bytes 32784
  227.3 0.9 copy.18
  228.2 2.9 convolution_negate_fusion.2
  231.1 1.9 fusion.33
  233.0 2.7 fusion.34
  235.7 110.8 %reduce-scatter.12.cloned.1.call-done = f32[16,512]{1,0:T(8,128)} async-done(((f32[512,512]{1,0:T(8,128)}), f32[16,512]{1,0:T(8,128)}) %reduce-scatter.12.cloned.1.call-update) | async-done | bytes 32784 | tf_op jit(solution)/shard_map/reduce_scatter | solution.py:78
  346.5 64.2 %all-gather.3.cloned.1.call-done = f32[2,512,512]{2,1,0:T(8,128)} async-done(((f32[2,16,512]{2,1,0:T(8,128)}), f32[2,512,512]{2,1,0:T(8,128)}) %all-gather.3.cloned.1.call-update) | async-done | bytes 2097168 | tf_op jit(solution)/shard_map/all_gather | solution.py:56
  410.7 2.0 fusion.13
  412.7 2.8 convolution_negate_fusion.1
  415.5 115.7 %reduce-scatter.14.cloned.1.call-done = f32[16,512]{1,0:T(8,128)} async-done(((f32[512,512]{1,0:T(8,128)}), f32[16,512]{1,0:T(8,128)}) %reduce-scatter.14.cloned.1.call-update) | async-done | bytes 32784 | tf_op jit(solution)/shard_map/reduce_scatter | solution.py:78
  531.2 1.4 fusion.11
  532.5 2.8 convolution_negate_fusion
  536.4 125.9 %all-reduce.9.cloned.1.call-done = (f32[512,512]{1,0:T(8,128)}, f32[512,512]{1,0:T(8,128)}, f32[512,512]{1,0:T(8,128)}, f32[512,512]{1,0:T(8,128)}, f32[512,512]{1,0:T(8,128)}) async-done(((f32[512,512]{1,0:T(8,128)}, f32[512,512]{1,0:T(8,128)}, f32[512,512]{1,0:T(8,128)}, f32[512,512]{1,0:T(8,128)}, f32[512,512]{1,0:T(8,128)}), (f32[512,512]{1,0:T(8,128)}, f32[512,512]{1,0:T(8,128)}, f32[512,512]{1,0:T(8,128)}, ...) | async-done | bytes 5242896 | tf_op jit(solution)/shard_map/psum | solution.py:38
  663.1 1.1 fusion.64
  664.2 66.6 %all-gather.5.cloned.1.call-done = f32[3,512,512]{2,1,0:T(8,128)} async-done(((f32[3,16,512]{2,1,0:T(8,128)}), f32[3,512,512]{2,1,0:T(8,128)}) %all-gather.5.cloned.1.call-update) | async-done | bytes 3145744 | tf_op jit(solution)/shard_map/all_gather | solution.py:55
  730.8 3.0 fusion.63
  733.8 244.1 %all-reduce.7.cloned.1.call-done = (f32[512,512]{1,0:T(8,128)}, f32[512,512]{1,0:T(8,128)}, f32[512,512]{1,0:T(8,128)}, f32[512,512]{1,0:T(8,128)}, f32[512,512]{1,0:T(8,128)}) async-done(((f32[512,512]{1,0:T(8,128)}, f32[512,512]{1,0:T(8,128)}, f32[512,512]{1,0:T(8,128)}, f32[512,512]{1,0:T(8,128)}, f32[512,512]{1,0:T(8,128)}), (f32[512,512]{1,0:T(8,128)}, f32[512,512]{1,0:T(8,128)}, f32[512,512]{1,0:T(8,128)}, ...) | async-done | bytes 5242896 | tf_op jit(solution)/shard_map/psum | solution.py:37
  977.9 1.9 fusion.14
  981.9 0.7 fusion.23
  984.5 1.4 fusion.9
  985.9 1.4 fusion.6
  (52 shorter events, 7.8 us)
Async XLA Ops:
  7.2 96.5 %copy-start = (f32[512,128]{1,0:T(8,128)S(1)}, f32[512,128]{1,0:T(8,128)}, u32[]{:S(2)}) copy-start(f32[512,128]{1,0:T(8,128)} %param.5) | copy-start | bytes 786436
  7.2 96.5 %all-reduce.11.cloned.1.call-start = ((), (), s32[]{:S(2)}) async-start(), calls=%async_computation.10 | async-start | bytes 1572864 | tf_op jit(solution)/shard_map/psum | solution.py:9
  10.3 1.1 copy-start.4
  10.3 1.9 copy-start.5
  10.3 220.8 %copy-start.3 = (f32[512,512]{1,0:T(8,128)}, f32[512,512]{1,0:T(8,128)S(1)}, u32[]{:S(2)}) copy-start(f32[512,512]{1,0:T(8,128)S(1)} %get-tuple-element.26) | copy-start | bytes 3145732
  12.2 215.1 %reduce-scatter.10.cloned.1.call-start = ((), (), s32[]{:S(2)}) async-start(), calls=%async_computation.5 | async-start | bytes 1081344
  103.7 3.5 copy-start.9
  107.1 239.3 %reduce-scatter.12.cloned.1.call-start = ((), (), s32[]{:S(2)}) async-start(), calls=%async_computation.6 | async-start | bytes 1081344 | tf_op jit(solution)/shard_map/reduce_scatter | solution.py:78
  107.2 3.0 copy-start.8
  109.6 301.1 %all-gather.3.cloned.1.call-start = ((), (), s32[]{:S(2)}) async-start(), calls=%async_computation.3 | async-start | bytes 2162688 | tf_op jit(solution)/shard_map/all_gather | solution.py:56
  110.2 421.0 %reduce-scatter.14.cloned.1.call-start = ((), (), s32[]{:S(2)}) async-start(), calls=%async_computation.7 | async-start | bytes 1081344 | tf_op jit(solution)/shard_map/reduce_scatter | solution.py:78
  112.6 549.7 %all-reduce.9.cloned.1.call-start = ((), (), s32[]{:S(2)}) async-start(), calls=%async_computation.9 | async-start | bytes 10485760 | tf_op jit(solution)/shard_map/psum | solution.py:38
  410.7 120.5 %copy-start.1 = (f32[2,512,512]{2,1,0:T(8,128)S(1)}, f32[2,512,512]{2,1,0:T(8,128)}, u32[]{:S(2)}) copy-start(f32[2,512,512]{2,1,0:T(8,128)} %all-gather.3.cloned.1.call-done) | copy-start | bytes 6291460
  535.4 195.4 %all-gather.5.cloned.1.call-start = ((), (), s32[]{:S(2)}) async-start(), calls=%async_computation.4 | async-start | bytes 3244032 | tf_op jit(solution)/shard_map/all_gather | solution.py:55
  536.2 441.7 %all-reduce.7.cloned.1.call-start = ((), (), s32[]{:S(2)}) async-start(), calls=%async_computation.8 | async-start | bytes 10485760 | tf_op jit(solution)/shard_map/psum | solution.py:37
  977.9 1.9 copy-start.2
  977.9 2.6 copy-start.7
  979.8 2.1 copy-start.6
Sparse Core Ops, SparseCore 0:
  12.3 91.3 all-reduce.10
  107.2 120.0 reduce-scatter.9
  229.8 116.5 reduce-scatter.11
  348.2 62.4 all-gather.2
  413.1 118.0 reduce-scatter.13
  535.5 126.7 all-reduce.8
  664.2 66.5 all-gather.4
  733.8 243.9 all-reduce.6
